TPU v7x, 512 devices: a whole 4x8x8 slice. The times are simulated.
512 devices in a mesh: row: 32 (over z, y_lo), col: 4 (over y_hi, core), head: 4 (over x).
Axes of the slice: x: 4, y: 8 (y_hi: 2, y_lo: 4; y = y_hi * 4 + y_lo), z: 8, core: 2. Of those that a mesh axis runs over, the one named last changes fastest.
Arguments:
- tokens: bfloat16 [512, 128, 1024], P(('row', 'head'), 'col'), may hold values from -6 to 6
- valid: int32 [512, 128], P('row', 'col'), may hold values 0 or 1
- gain: float32 [1024], replicated, may hold values from 0.1 to 1.9
- w_qkv: bfloat16 [1024, 3, 1024], P(None, None, 'head'), may hold values from -0.1875 to 0.1875
- w_proj: bfloat16 [1024, 1024], P('head'), may hold values from -0.1875 to 0.1875
- rel_table: float32 [225, 16], P(None, 'head'), may hold values from -4 to 300
- cotangent: bfloat16 [512, 128, 1024], P(('row', 'head'), 'col'), may hold values from -24 to 24
Outputs:
- mixed: bfloat16 [512, 128, 1024], P(('row', 'head'), 'col')
- token_gradient: bfloat16 [512, 128, 1024], P(('row', 'head'), 'col')
- proj_grad: float32 [1024, 1024], P('head', ('row', 'col'))
- table_grad: float32 [225, 16], P(None, 'head')
All inputs are finite; a program needn't handle non-finite values. No bound on the sum of `valid` on one device may be relied on, other than what follows from the above.
Results may differ from a plain program's by a relative error of at most 0.0078.
Values may be sent and summed in bfloat16 or wider, within the bound.
No kernel may reach another device: no remote copies, remote signals or barrier semaphores. Data moves between devices by JAX's collectives and lax.ppermute only.
A program may use at most 64 MiB of HBM per device.

v0:
```python
import math
import jax
import jax.numpy as jnp
from jax import lax
from jax.sharding import PartitionSpec as P

HD = 64
WIN = 8
SHIFT = 4
EPS = 1e-05
HIGH = lax.Precision.HIGHEST


def passed_along(value, axis, steps):
    count = lax.axis_size(axis)
    pairs = [(source, (source + steps) % count) for source in range(count)]
    return lax.ppermute(value, axis, pairs)


def region(index, grand_total):
    return jnp.where(
        index < grand_total - WIN, 0, jnp.where(index < grand_total - SHIFT, 1, 2)
    ).astype(jnp.int32)


def offsets():
    span = 2 * WIN - 1
    pos = jnp.arange(WIN * WIN, dtype=jnp.int32)
    prow = pos // WIN
    pcol = pos % WIN
    index = (prow[:, None] - prow[None, :] + WIN - 1) * span + (
        pcol[:, None] - pcol[None, :] + WIN - 1
    )
    table_ids = jnp.arange(span * span, dtype=jnp.int32)
    return (
        (index[:, :, None] == table_ids[None, None, :])
        .astype(jnp.float32)
        .reshape(WIN * WIN * WIN * WIN, span * span)
    )


def to_windows(block):
    nrow, ncol, heads, depth = block.shape
    block = block.reshape(nrow // WIN, WIN, ncol // WIN, WIN, heads, depth).transpose(
        0, 2, 4, 1, 3, 5
    )
    return block.reshape(nrow // WIN * (ncol // WIN), heads, WIN * WIN, depth)


def from_windows(block, nrow, ncol):
    count, heads, posn, depth = block.shape
    block = block.reshape(nrow // WIN, ncol // WIN, heads, WIN, WIN, depth).transpose(
        0, 3, 1, 4, 2, 5
    )
    return block.reshape(nrow, ncol, heads * depth)


def rows_in(block):
    return jnp.concatenate([block[SHIFT:], passed_along(block[:SHIFT], "row", -1)], 0)


def cols_in(block):
    return jnp.concatenate([block[:, SHIFT:], passed_along(block[:, :SHIFT], "col", -1)], 1)


def rows_out(block):
    return jnp.concatenate([passed_along(block[-SHIFT:], "row", 1), block[:-SHIFT]], 0)


def cols_out(block):
    return jnp.concatenate([passed_along(block[:, -SHIFT:], "col", 1), block[:, :-SHIFT]], 1)


def roll_in(block):
    return cols_in(rows_in(block))


def roll_out(block):
    return cols_out(rows_out(block))


def roll_pair(first, second, roller):
    return (roller(first), roller(second))


def head_sum(term_fn, part_rows):
    return lax.psum_scatter(
        term_fn(jnp.int32(0), lax.axis_size("head") * part_rows).astype(jnp.bfloat16),
        "head",
        scatter_dimension=0,
        tiled=True,
    ).astype(jnp.float32)


def attend(qkv, grad, labels, valid, bias, onehot):
    nrow, ncol = labels.shape
    feature_width = qkv.shape[3]
    heads = feature_width // HD
    scale = HD ** (-0.5)
    f32 = jnp.float32
    query = to_windows(qkv[:, :, 0].reshape(nrow, ncol, heads, HD))
    key = to_windows(qkv[:, :, 1].reshape(nrow, ncol, heads, HD))
    value = to_windows(qkv[:, :, 2].reshape(nrow, ncol, heads, HD))
    dout = to_windows(grad.reshape(nrow, ncol, heads, HD))
    lab_win = to_windows(labels[:, :, None, None])[:, 0, :, 0]
    val_win = to_windows(valid[:, :, None, None])[:, 0, :, 0]
    diagonal = jnp.eye(WIN * WIN, dtype=bool)
    allowed = (lab_win[:, :, None] == lab_win[:, None, :]) & (
        (val_win[:, None, :] == 1) | diagonal[None]
    )
    scores = (
        jnp.einsum("wiqd,wikd->wiqk", query, key, preferred_element_type=f32) * scale + bias[None]
    )
    scores = jnp.where(allowed[:, None], scores, -1e30)
    top = jnp.max(scores, -1, keepdims=True)
    expo = jnp.exp(scores - top)
    prob = expo / jnp.sum(expo, -1, keepdims=True)
    prob_b = prob.astype(jnp.bfloat16)
    attended = jnp.einsum("wiqk,wikd->wiqd", prob_b, value, preferred_element_type=f32).astype(
        jnp.bfloat16
    )
    dprob = jnp.einsum("wiqd,wikd->wiqk", dout, value, preferred_element_type=f32)
    dvalue = jnp.einsum("wiqk,wiqd->wikd", prob_b, dout, preferred_element_type=f32).astype(
        jnp.bfloat16
    )
    dscore = prob * (dprob - jnp.sum(prob * dprob, -1, keepdims=True))
    dscore_b = dscore.astype(jnp.bfloat16)
    dquery = (
        jnp.einsum("wiqk,wikd->wiqd", dscore_b, key, preferred_element_type=f32) * scale
    ).astype(jnp.bfloat16)
    dkey = (
        jnp.einsum("wiqk,wiqd->wikd", dscore_b, query, preferred_element_type=f32) * scale
    ).astype(jnp.bfloat16)
    summed = jnp.sum(dscore, 0).transpose(1, 2, 0).reshape(WIN * WIN * WIN * WIN, heads)
    tgrad = jnp.dot(onehot.T, summed, precision=HIGH)
    grads = jnp.stack(
        [
            from_windows(dquery, nrow, ncol),
            from_windows(dkey, nrow, ncol),
            from_windows(dvalue, nrow, ncol),
        ],
        2,
    )
    return (from_windows(attended, nrow, ncol), grads, tgrad)


def on_device(tokens, valid, gain, w_qkv, w_proj, rel_table, cotangent):
    part_rows, ncol, feature_width = tokens.shape
    tile_rows = part_rows * lax.axis_size("head")
    row_count = lax.axis_size("row")
    col_count = lax.axis_size("col")
    flat = tokens.astype(jnp.float32)
    token_average = jnp.mean(flat, -1, keepdims=True)
    centered_input = flat - token_average
    inverse_deviation = lax.rsqrt(
        jnp.mean(centered_input * centered_input, -1, keepdims=True) + EPS
    )
    standardized_input = centered_input * inverse_deviation
    normalized_tokens = (standardized_input * gain).astype(jnp.bfloat16)
    grad_tile = lax.all_gather(cotangent, "head", axis=0, tiled=True)
    out_grad = jnp.einsum(
        "rcd,nd->rcn", grad_tile, w_proj, preferred_element_type=jnp.float32
    ).astype(jnp.bfloat16)
    source = lax.all_gather(normalized_tokens, "head", axis=0, tiled=True)
    moved, rolled_grad = roll_pair(source, out_grad, roll_in)
    rolled = jnp.einsum("rcd,dtn->rctn", moved, w_qkv, preferred_element_type=jnp.float32).astype(
        jnp.bfloat16
    )
    row_lab = region(
        lax.axis_index("row") * tile_rows + jnp.arange(tile_rows, dtype=jnp.int32),
        tile_rows * row_count,
    )
    col_lab = region(
        lax.axis_index("col") * ncol + jnp.arange(ncol, dtype=jnp.int32), ncol * col_count
    )
    labels = 3 * row_lab[:, None] + col_lab[None, :]
    onehot = offsets()
    heads = rel_table.shape[1]
    bias = (
        jnp.dot(onehot, rel_table, precision=HIGH)
        .reshape(WIN * WIN, WIN * WIN, heads)
        .transpose(2, 0, 1)
    )
    attended, grads, tgrad = attend(rolled, rolled_grad, labels, valid, bias, onehot)
    attn_out, qkv_grad = roll_pair(attended, grads, roll_out)

    def proj_term(start, count):
        return jnp.einsum("rcn,nd->rcd", attn_out, w_proj, preferred_element_type=jnp.float32)

    def back_term(start, count):
        return jnp.einsum("rctn,dtn->rcd", qkv_grad, w_qkv, preferred_element_type=jnp.float32)

    mixed = (flat + head_sum(proj_term, part_rows)).astype(jnp.bfloat16)
    norm_grad = head_sum(back_term, part_rows)
    scale = 1.0 / math.sqrt(tile_rows * ncol * row_count * col_count)
    weight_term = jnp.einsum("rcn,rcd->nd", attn_out, grad_tile, preferred_element_type=jnp.float32)
    proj_grad = (
        lax.psum_scatter(weight_term, ("row", "col"), scatter_dimension=1, tiled=True) * scale
    )
    table_grad = lax.psum(tgrad, ("row", "col")) * (WIN * scale)
    scaled_tokens = norm_grad * gain
    token_gradient = cotangent.astype(jnp.float32) + inverse_deviation * (
        scaled_tokens
        - jnp.mean(scaled_tokens, -1, keepdims=True)
        - standardized_input * jnp.mean(scaled_tokens * standardized_input, -1, keepdims=True)
    )
    return (mixed, token_gradient.astype(jnp.bfloat16), proj_grad, table_grad)


def solution(mesh):
    return jax.shard_map(
        on_device,
        mesh=mesh,
        in_specs=(
            P(("row", "head"), "col", None),
            P("row", "col"),
            P(),
            P(None, None, "head"),
            P("head", None),
            P(None, "head"),
            P(("row", "head"), "col", None),
        ),
        out_specs=(
            P(("row", "head"), "col", None),
            P(("row", "head"), "col", None),
            P("head", ("row", "col")),
            P(None, "head"),
        ),
        check_vma=False,
    )
```

profile of v0, /device:TPU:8, one launch (start us, length us, event | category | flops | bytes accessed | tf_op | source)
XLA Modules:
  0.0 753.7 jit_solution(1386446947580851297)
XLA Ops:
  10.2 1.9 fusion.30
  14.0 3.4 fusion.17
  17.5 28.7 %all-gather.3.cloned.1.call-done = bf16[16,32,1024]{2,1,0:T(8,128)(2,1)} async-done(((bf16[4,32,1024]{2,1,0:T(8,128)(2,1)}), bf16[16,32,1024]{2,1,0:T(8,128)(2,1)}) %all-gather.3.cloned.1.call-update) | async-done | bytes 1048592 | tf_op jit(solution)/shard_map/all_gather | solution.py:164
  46.2 1.8 slice.77
  47.9 2.4 collective-permute-start
  50.4 27.6 %all-gather.5.cloned.1.call-done = bf16[16,32,1024]{2,1,0:T(8,128)(2,1)} async-done(((bf16[4,32,1024]{2,1,0:T(8,128)(2,1)}), bf16[16,32,1024]{2,1,0:T(8,128)(2,1)}) %all-gather.5.cloned.1.call-update) | async-done | bytes 1048592 | tf_op jit(solution)/shard_map/all_gather | solution.py:160
  78.0 1.7 convolution_convert_fusion.3
  79.7 2.4 collective-permute-start.4
  86.5 4.2 collective-permute-start.5
  91.5 4.3 collective-permute-start.1
  96.1 2.2 collective-permute-done.1
  106.7 3.0 convolution_convert_fusion.2
  109.7 1.7 copy.46
  113.3 2.5 collective-permute-start.2
  115.8 1.7 pad_maximum_fusion.2
  120.9 4.4 collective-permute-start.3
  125.4 2.9 convolution_convert_fusion.1
  128.3 1.7 copy.55
  131.1 2.8 convolution_bitcast_fusion
  134.2 1.9 multiply_reduce_fusion
  138.9 1.5 copy.54
  140.4 2.2 stack_reshape.10
  144.4 6.4 collective-permute-start.6
  150.8 7.1 collective-permute-done.6
  157.9 2.4 collective-permute-start.7
  160.3 7.9 %collective-permute-done.7 = bf16[16,4,3,256]{3,1,2,0:T(4,128)(2,1)S(1)} collective-permute-done((bf16[16,4,3,256]{3,1,2,0:T(4,128)(2,1)S(1)}, bf16[16,4,3,256]{3,1,2,0:T(4,128)(2,1)S(1)}, u32[]{:S(2)}, u32[]{:S(2)}) %collective-permute-start.7) | collective-permute-done | bytes 98336 | tf_op jit(solution)/shard_map/ppermute | solution.py:17
  168.2 2.0 bitcast_convert_fusion
  173.4 266.7 %psum.7 = f32[225,4]{0,1:T(4,128)S(1)} all-reduce(f32[225,4]{0,1:T(4,128)S(1)} %fusion.18), channel_id=1, replica_groups=mesh['row'=32,'col'=4,'head'=4] {'row','col'}, use_global_device_ids=true, to_apply=%region_11.12 | all-reduce | flops 900 | bytes 7200 | tf_op jit(solution)/shard_map/psum | solution.py:200
  440.7 237.8 %reduce-scatter.8.cloned.1.call-done = f32[256,8]{0,1:T(8,128)} async-done(((f32[256,1024]{0,1:T(8,128)}), f32[256,8]{0,1:T(8,128)}) %reduce-scatter.8.cloned.1.call-update) | async-done | bytes 8208 | tf_op jit(solution)/shard_map/reduce_scatter | solution.py:198
  679.8 34.0 %reduce-scatter.6.cloned.1.call-done = bf16[4,32,1024]{2,1,0:T(8,128)(2,1)} async-done(((bf16[16,32,1024]{2,1,0:T(8,128)(2,1)}), bf16[4,32,1024]{2,1,0:T(8,128)(2,1)}) %reduce-scatter.6.cloned.1.call-update) | async-done | bytes 262160 | tf_op jit(solution)/shard_map/reduce_scatter | solution.py:87
  715.0 30.1 %reduce-scatter.4.cloned.1.call-done = bf16[4,32,1024]{2,1,0:T(8,128)(2,1)} async-done(((bf16[16,32,1024]{2,1,0:T(8,128)(2,1)}), bf16[4,32,1024]{2,1,0:T(8,128)(2,1)}) %reduce-scatter.4.cloned.1.call-update) | async-done | bytes 262160 | tf_op jit(solution)/shard_map/reduce_scatter | solution.py:87
  745.1 2.1 fusion.35
  (123 shorter events, 36.1 us)
Async XLA Ops:
  7.2 91.1 %copy-start = (bf16[1024,3,256]{2,0,1:T(8,128)(2,1)S(1)}, bf16[1024,3,256]{2,0,1:T(8,128)(2,1)}, u32[]{:S(2)}) copy-start(bf16[1024,3,256]{2,0,1:T(8,128)(2,1)} %param.10) | copy-start | bytes 4718596
  7.2 5.9 copy-start.21
  7.2 6.8 copy-start.22
  7.2 38.9 %all-gather.3.cloned.1.call-start = ((), (), s32[]{:S(2)}) async-start(), calls=%async_computation.3 | async-start | bytes 1310720 | tf_op jit(solution)/shard_map/all_gather | solution.py:164
  8.4 1.3 copy-start.14
  8.4 69.5 %copy-start.8 = (bf16[256,1024]{1,0:T(8,128)(2,1)S(1)}, bf16[256,1024]{1,0:T(8,128)(2,1)}, u32[]{:S(2)}) copy-start(bf16[256,1024]{1,0:T(8,128)(2,1)} %param.11) | copy-start | bytes 1572868
  12.1 65.8 %all-gather.5.cloned.1.call-start = ((), (), s32[]{:S(2)}) async-start(), calls=%async_computation.5 | async-start | bytes 1310720 | tf_op jit(solution)/shard_map/all_gather | solution.py:160
  12.9 665.6 %reduce-scatter.8.cloned.1.call-start = ((), (), s32[]{:S(2)}) async-start(), calls=%async_computation.7 | async-start | bytes 1056768 | tf_op jit(solution)/shard_map/reduce_scatter | solution.py:198
  46.1 38.2 %copy-start.6 = (bf16[16,32,1024]{2,1,0:T(8,128)(2,1)S(1)}, bf16[16,32,1024]{2,1,0:T(8,128)(2,1)}, u32[]{:S(2)}) copy-start(bf16[16,32,1024]{2,1,0:T(8,128)(2,1)} %all-gather.3.cloned.1.call-done) | copy-start | bytes 3145732
  47.9 43.5 %collective-permute-start = (bf16[4,32,1024]{2,1,0:T(8,128)(2,1)}, bf16[4,32,1024]{2,1,0:T(8,128)(2,1)S(1)}, u32[]{:S(2)}, u32[]{:S(2)}) collective-permute-start(bf16[4,32,1024]{2,1,0:T(8,128)(2,1)} %slice.77), channel_id=1, source_target_pairs={{0,496},{16,0},{32,16},{48,32},{64,48},{80,64},{96,80},{112,96},{1... | collective-permute-start | bytes 786440 | tf_op jit(solution)/shard_map/ppermute | solution.py:17
  79.7 2.5 copy-start.11
  79.7 6.2 collective-permute-start.4
  86.5 29.3 %collective-permute-start.5 = (bf16[16,4,256]{2,1,0:T(4,128)(2,1)}, bf16[16,4,256]{2,1,0:T(4,128)(2,1)}, u32[]{:S(2)}, u32[]{:S(2)}) collective-permute-start(bf16[16,4,256]{2,1,0:T(4,128)(2,1)} %pad_maximum_fusion.5), channel_id=1, source_target_pairs={{0,12},{4,0},{8,4},{12,8},{1,13},{5,1},{9,5},{13,9},{2,14},{6,2},{... | collective-permute-start | bytes 98312 | tf_op jit(solution)/shard_map/ppermute | solution.py:17
  91.5 6.8 collective-permute-start.1
  113.3 7.6 %collective-permute-start.2 = (bf16[4,32,256]{2,1,0:T(8,128)(2,1)S(1)}, bf16[4,32,256]{2,1,0:T(8,128)(2,1)S(1)}, u32[]{:S(2)}, u32[]{:S(2)}) collective-permute-start(bf16[4,32,256]{2,1,0:T(8,128)(2,1)S(1)} %slice.83), channel_id=1, source_target_pairs={{0,16},{16,32},{32,48},{48,64},{64,80},{80,96},{96,112},{112,128},... | collective-permute-start | bytes 196616 | tf_op jit(solution)/shard_map/ppermute | solution.py:17
  120.9 10.1 %collective-permute-start.3 = (bf16[16,4,256]{2,1,0:T(4,128)(2,1)S(1)}, bf16[16,4,256]{2,1,0:T(4,128)(2,1)S(1)}, u32[]{:S(2)}, u32[]{:S(2)}) collective-permute-start(bf16[16,4,256]{2,1,0:T(4,128)(2,1)S(1)} %pad_maximum_fusion.6), channel_id=1, source_target_pairs={{0,4},{4,8},{8,12},{12,0},{1,5},{5,9},{9,13},{13,1},{2,6},{6,10},{... | collective-permute-start | bytes 98312 | tf_op jit(solution)/shard_map/ppermute | solution.py:17
  131.1 3.1 copy-start.10
  131.1 2.8 copy-start.12
  133.9 579.8 %reduce-scatter.6.cloned.1.call-start = ((), (), s32[]{:S(2)}) async-start(), calls=%async_computation.6 | async-start | bytes 1310720 | tf_op jit(solution)/shard_map/reduce_scatter | solution.py:87
  134.2 1.9 copy-start.2
  142.9 1.4 copy-start.5
  144.4 13.5 %collective-permute-start.6 = (bf16[4,32,3,256]{3,1,2,0:T(8,128)(2,1)S(1)}, bf16[4,32,3,256]{3,1,2,0:T(8,128)(2,1)S(1)}, u32[]{:S(2)}, u32[]{:S(2)}) collective-permute-start(bf16[4,32,3,256]{3,1,2,0:T(8,128)(2,1)S(1)} %slice.89), channel_id=1, source_target_pairs={{0,16},{16,32},{32,48},{48,64},{64,80},{80,96},{96,112},{112,128},... | collective-permute-start | bytes 589832 | tf_op jit(solution)/shard_map/ppermute | solution.py:17
  157.9 12.4 %copy-start.9 = (bf16[256,1024]{1,0:T(8,128)(2,1)S(1)}, bf16[256,1024]{1,0:T(8,128)(2,1)}, u32[]{:S(2)}) copy-start(bf16[256,1024]{1,0:T(8,128)(2,1)} %param.11) | copy-start | bytes 1572868
  157.9 12.4 %copy-start.13 = (bf16[16,4,256]{2,1,0:T(4,128)(2,1)S(1)}, bf16[16,4,256]{2,1,0:T(4,128)(2,1)}, u32[]{:S(2)}) copy-start(bf16[16,4,256]{2,1,0:T(4,128)(2,1)} %copy-done.12) | copy-start | bytes 98308
  157.9 10.3 %collective-permute-start.7 = (bf16[16,4,3,256]{3,1,2,0:T(4,128)(2,1)S(1)}, bf16[16,4,3,256]{3,1,2,0:T(4,128)(2,1)S(1)}, u32[]{:S(2)}, u32[]{:S(2)}) collective-permute-start(bf16[16,4,3,256]{3,1,2,0:T(4,128)(2,1)S(1)} %pad_maximum_fusion.4), channel_id=1, source_target_pairs={{0,4},{4,8},{8,12},{12,0},{1,5},{5,9},{9,13},{13,1},{2,6},{6,10},{... | collective-permute-start | bytes 294920 | tf_op jit(solution)/shard_map/ppermute | solution.py:17
  170.3 1.7 copy-start.20
  170.3 574.9 %reduce-scatter.4.cloned.1.call-start = ((), (), s32[]{:S(2)}) async-start(), calls=%async_computation.4 | async-start | bytes 1310720 | tf_op jit(solution)/shard_map/reduce_scatter | solution.py:87
  171.8 542.0 %copy-start.1 = (bf16[4,32,1024]{2,1,0:T(8,128)(2,1)S(1)}, bf16[4,32,1024]{2,1,0:T(8,128)(2,1)}, u32[]{:S(2)}) copy-start(bf16[4,32,1024]{2,1,0:T(8,128)(2,1)} %param.7) | copy-start | bytes 786436
  171.8 542.0 %copy-start.15 = (f32[4,32]{1,0:T(4,128)S(1)}, f32[4,32]{1,0:T(4,128)}, u32[]{:S(2)}) copy-start(f32[4,32]{1,0:T(4,128)} %copy-done.14) | copy-start | bytes 1540
  171.8 542.0 %copy-start.16 = (f32[1024]{0:T(1024)S(1)}, f32[1024]{0:T(1024)}, u32[]{:S(2)}) copy-start(f32[1024]{0:T(1024)} %param.9) | copy-start | bytes 12292
  171.8 542.0 %copy-start.18 = (f32[4,32]{1,0:T(4,128)S(1)}, f32[4,32]{1,0:T(4,128)}, u32[]{:S(2)}) copy-start(f32[4,32]{1,0:T(4,128)} %copy-done.17) | copy-start | bytes 1540
  171.8 573.3 %copy-start.7 = (bf16[4,32,1024]{2,1,0:T(8,128)(2,1)S(1)}, bf16[4,32,1024]{2,1,0:T(8,128)(2,1)}, u32[]{:S(2)}) copy-start(bf16[4,32,1024]{2,1,0:T(8,128)(2,1)} %param.13) | copy-start | bytes 786436
  (4 other events, 3.2 us)
Sparse Core Ops, SparseCore 0:
  12.3 33.8 all-gather.2
  48.2 29.6 all-gather.4
  134.0 544.4 reduce-scatter.7
  681.4 32.2 reduce-scatter.5
  716.4 28.6 reduce-scatter.3
where the time goes:
time: 755 us; the launch traced here: 754 us
  waiting for transfers between devices  378 us (50%)
  blocking collectives  267 us (35%)
  starting transfers between devices  29.4 us (4%)
  local copies, waits for them, and re-layouts  26.9 us (4%)
  matrix products  23.6 us (3%)
  other arithmetic  14.9 us (2%)
  between operations  14.4 us (2%)
    psum x1, blocking collectives, on_device(): table_grad = lax.psum(tgrad, ('row', 'col')) * (WIN * scale)  267 us
    reduce_scatter x1, waiting for transfers between devices, on_device(): lax.psum_scatter(weight_term, ('row', 'col'), scatter_dimension=1, tiled=...  238 us
    reduce_scatter x2, waiting for transfers between devices, head_sum(): lax.psum_scatter(term_fn(jnp.int32(0), lax.axis_size('head') * part_rows)...  64.1 us
    ppermute x8, starting transfers between devices, passed_along(): return lax.ppermute(value, axis, pairs)  29 us
    all_gather x1, waiting for transfers between devices, on_device(): source = lax.all_gather(normalized_tokens, 'head', axis=0, tiled=True)  28.7 us
    all_gather x1, waiting for transfers between devices, on_device(): grad_tile = lax.all_gather(cotangent, 'head', axis=0, tiled=True)  27.6 us
    ppermute x8, waiting for transfers between devices, passed_along(): return lax.ppermute(value, axis, pairs)  19 us
  transfers between devices with their start and end apart: 13, of which 10 were waited for; matrix products, arithmetic and copies ran while one was open for 7% of the time, Pallas kernels for 0%

commit v1 on v0

--- a/solution.py
+++ b/solution.py
@@ -9,6 +9,10 @@
 SHIFT = 4
 EPS = 1e-05
 HIGH = lax.Precision.HIGHEST
+
+
+def touch_chunk_on_mesh(vec):
+    return lax.psum(lax.psum(vec, "col"), axis_name="row")
 
 
 def passed_along(value, axis, steps):
@@ -197,7 +201,7 @@
     proj_grad = (
         lax.psum_scatter(weight_term, ("row", "col"), scatter_dimension=1, tiled=True) * scale
     )
-    table_grad = lax.psum(tgrad, ("row", "col")) * (WIN * scale)
+    table_grad = touch_chunk_on_mesh(tgrad) * (WIN * scale)
     scaled_tokens = norm_grad * gain
     token_gradient = cotangent.astype(jnp.float32) + inverse_deviation * (
         scaled_tokens

time: 755 us -> 755 us (level)
  blocking collectives: 267 us -> 90 us
  waiting for transfers between devices: 378 us -> 555 us
    psum x1 -> x2, blocking collectives: 267 us -> 90 us  [touch_chunk_on_mesh(): return lax.psum(lax.psum(vec, 'col'), axis_name='row')]
    reduce_scatter x1, waiting for transfers between devices: 238 us -> 414 us  [on_device(): lax.psum_scatter(weight_term, ('row', 'col'), scatter_dimension=1, tiled=...]
where the time goes in v1:
time: 755 us; the launch traced here: 754 us
  waiting for transfers between devices  555 us (74%)
  blocking collectives  90 us (12%)
  starting transfers between devices  29.4 us (4%)
  local copies, waits for them, and re-layouts  26.9 us (4%)
  matrix products  23.5 us (3%)
  other arithmetic  14.9 us (2%)
  between operations  14.4 us (2%)
    reduce_scatter x1, waiting for transfers between devices, on_device(): lax.psum_scatter(weight_term, ('row', 'col'), scatter_dimension=1, tiled=...  414 us
    psum x2, blocking collectives, touch_chunk_on_mesh(): return lax.psum(lax.psum(vec, 'col'), axis_name='row')  90 us
    reduce_scatter x2, waiting for transfers between devices, head_sum(): lax.psum_scatter(term_fn(jnp.int32(0), lax.axis_size('head') * part_rows)...  64.8 us
    ppermute x8, starting transfers between devices, passed_along(): return lax.ppermute(value, axis, pairs)  29 us
    all_gather x1, waiting for transfers between devices, on_device(): source = lax.all_gather(normalized_tokens, 'head', axis=0, tiled=True)  28.7 us
    all_gather x1, waiting for transfers between devices, on_device(): grad_tile = lax.all_gather(cotangent, 'head', axis=0, tiled=True)  27.6 us
    ppermute x8, waiting for transfers between devices, passed_along(): return lax.ppermute(value, axis, pairs)  19 us
  transfers between devices with their start and end apart: 13, of which 10 were waited for; matrix products, arithmetic and copies ran while one was open for 7% of the time, Pallas kernels for 0%

profile of v1, /device:TPU:8, one launch (start us, length us, event | category | flops | bytes accessed | tf_op | source)
XLA Modules:
  0.0 753.7 jit_solution(17927255244606524388)
XLA Ops:
  10.3 1.9 fusion.30
  14.1 3.4 fusion.17
  17.5 28.7 %all-gather.3.cloned.1.call-done = bf16[16,32,1024]{2,1,0:T(8,128)(2,1)} async-done(((bf16[4,32,1024]{2,1,0:T(8,128)(2,1)}), bf16[16,32,1024]{2,1,0:T(8,128)(2,1)}) %all-gather.3.cloned.1.call-update) | async-done | bytes 1048592 | tf_op jit(solution)/shard_map/all_gather | solution.py:168
  46.2 1.8 slice.77
  48.0 2.4 collective-permute-start
  50.4 27.6 %all-gather.5.cloned.1.call-done = bf16[16,32,1024]{2,1,0:T(8,128)(2,1)} async-done(((bf16[4,32,1024]{2,1,0:T(8,128)(2,1)}), bf16[16,32,1024]{2,1,0:T(8,128)(2,1)}) %all-gather.5.cloned.1.call-update) | async-done | bytes 1048592 | tf_op jit(solution)/shard_map/all_gather | solution.py:164
  78.0 1.7 convolution_convert_fusion.3
  79.7 2.4 collective-permute-start.4
  86.5 4.2 collective-permute-start.5
  91.5 4.3 collective-permute-start.1
  96.1 2.2 collective-permute-done.1
  106.8 2.9 convolution_convert_fusion.2
  109.7 1.7 copy.46
  113.3 2.5 collective-permute-start.2
  115.8 1.7 pad_maximum_fusion.2
  120.9 4.5 collective-permute-start.3
  125.4 2.9 convolution_convert_fusion.1
  128.3 1.7 copy.55
  131.1 2.8 convolution_bitcast_fusion
  134.2 1.9 multiply_reduce_fusion
  140.5 2.2 stack_reshape.10
  144.4 6.3 collective-permute-start.6
  150.8 7.1 collective-permute-done.6
  158.0 2.4 collective-permute-start.7
  160.3 7.9 %collective-permute-done.7 = bf16[16,4,3,256]{3,1,2,0:T(4,128)(2,1)S(1)} collective-permute-done((bf16[16,4,3,256]{3,1,2,0:T(4,128)(2,1)S(1)}, bf16[16,4,3,256]{3,1,2,0:T(4,128)(2,1)S(1)}, u32[]{:S(2)}, u32[]{:S(2)}) %collective-permute-start.7) | collective-permute-done | bytes 98336 | tf_op jit(solution)/shard_map/ppermute | solution.py:21
  168.3 2.0 bitcast_convert_fusion
  173.4 9.6 %psum.14 = f32[225,4]{0,1:T(4,128)S(1)} all-reduce(f32[225,4]{0,1:T(4,128)S(1)} %fusion.18), channel_id=1, replica_groups=mesh['row'=32,'col'=4,'head'=4] {'col'}, use_global_device_ids=true, to_apply=%region_11.12 | all-reduce | flops 900 | bytes 7200 | tf_op jit(solution)/shard_map/psum | solution.py:15
  183.0 80.4 %psum.15 = f32[225,4]{0,1:T(4,128)S(1)} all-reduce(f32[225,4]{0,1:T(4,128)S(1)} %psum.14), channel_id=1, replica_groups=mesh['row'=32,'col'=4,'head'=4] {'row'}, use_global_device_ids=true, to_apply=%region_12.13 | all-reduce | flops 900 | bytes 7200 | tf_op jit(solution)/shard_map/psum | solution.py:15
  264.0 413.7 %reduce-scatter.8.cloned.1.call-done = f32[256,8]{0,1:T(8,128)} async-done(((f32[256,1024]{0,1:T(8,128)}), f32[256,8]{0,1:T(8,128)}) %reduce-scatter.8.cloned.1.call-update) | async-done | bytes 8208 | tf_op jit(solution)/shard_map/reduce_scatter | solution.py:202
  679.0 34.7 %reduce-scatter.6.cloned.1.call-done = bf16[4,32,1024]{2,1,0:T(8,128)(2,1)} async-done(((bf16[16,32,1024]{2,1,0:T(8,128)(2,1)}), bf16[4,32,1024]{2,1,0:T(8,128)(2,1)}) %reduce-scatter.6.cloned.1.call-update) | async-done | bytes 262160 | tf_op jit(solution)/shard_map/reduce_scatter | solution.py:91
  715.0 30.1 %reduce-scatter.4.cloned.1.call-done = bf16[4,32,1024]{2,1,0:T(8,128)(2,1)} async-done(((bf16[16,32,1024]{2,1,0:T(8,128)(2,1)}), bf16[4,32,1024]{2,1,0:T(8,128)(2,1)}) %reduce-scatter.4.cloned.1.call-update) | async-done | bytes 262160 | tf_op jit(solution)/shard_map/reduce_scatter | solution.py:91
  745.1 2.1 fusion.35
  (124 shorter events, 37.6 us)
Async XLA Ops:
  7.2 91.2 %copy-start = (bf16[1024,3,256]{2,0,1:T(8,128)(2,1)S(1)}, bf16[1024,3,256]{2,0,1:T(8,128)(2,1)}, u32[]{:S(2)}) copy-start(bf16[1024,3,256]{2,0,1:T(8,128)(2,1)} %param.10) | copy-start | bytes 4718596
  7.2 6.0 copy-start.21
  7.2 6.9 copy-start.22
  7.2 39.0 %all-gather.3.cloned.1.call-start = ((), (), s32[]{:S(2)}) async-start(), calls=%async_computation.3 | async-start | bytes 1310720 | tf_op jit(solution)/shard_map/all_gather | solution.py:168
  8.4 1.3 copy-start.14
  8.4 69.6 %copy-start.8 = (bf16[256,1024]{1,0:T(8,128)(2,1)S(1)}, bf16[256,1024]{1,0:T(8,128)(2,1)}, u32[]{:S(2)}) copy-start(bf16[256,1024]{1,0:T(8,128)(2,1)} %param.11) | copy-start | bytes 1572868
  12.2 65.8 %all-gather.5.cloned.1.call-start = ((), (), s32[]{:S(2)}) async-start(), calls=%async_computation.5 | async-start | bytes 1310720 | tf_op jit(solution)/shard_map/all_gather | solution.py:164
  12.9 664.8 %reduce-scatter.8.cloned.1.call-start = ((), (), s32[]{:S(2)}) async-start(), calls=%async_computation.7 | async-start | bytes 1056768 | tf_op jit(solution)/shard_map/reduce_scatter | solution.py:202
  46.2 38.2 %copy-start.6 = (bf16[16,32,1024]{2,1,0:T(8,128)(2,1)S(1)}, bf16[16,32,1024]{2,1,0:T(8,128)(2,1)}, u32[]{:S(2)}) copy-start(bf16[16,32,1024]{2,1,0:T(8,128)(2,1)} %all-gather.3.cloned.1.call-done) | copy-start | bytes 3145732
  48.0 43.5 %collective-permute-start = (bf16[4,32,1024]{2,1,0:T(8,128)(2,1)}, bf16[4,32,1024]{2,1,0:T(8,128)(2,1)S(1)}, u32[]{:S(2)}, u32[]{:S(2)}) collective-permute-start(bf16[4,32,1024]{2,1,0:T(8,128)(2,1)} %slice.77), channel_id=1, source_target_pairs={{0,496},{16,0},{32,16},{48,32},{64,48},{80,64},{96,80},{112,96},{1... | collective-permute-start | bytes 786440 | tf_op jit(solution)/shard_map/ppermute | solution.py:21
  79.7 2.5 copy-start.11
  79.7 6.2 collective-permute-start.4
  86.5 29.3 %collective-permute-start.5 = (bf16[16,4,256]{2,1,0:T(4,128)(2,1)}, bf16[16,4,256]{2,1,0:T(4,128)(2,1)}, u32[]{:S(2)}, u32[]{:S(2)}) collective-permute-start(bf16[16,4,256]{2,1,0:T(4,128)(2,1)} %pad_maximum_fusion.5), channel_id=1, source_target_pairs={{0,12},{4,0},{8,4},{12,8},{1,13},{5,1},{9,5},{13,9},{2,14},{6,2},{... | collective-permute-start | bytes 98312 | tf_op jit(solution)/shard_map/ppermute | solution.py:21
  91.5 6.8 collective-permute-start.1
  113.3 7.6 %collective-permute-start.2 = (bf16[4,32,256]{2,1,0:T(8,128)(2,1)S(1)}, bf16[4,32,256]{2,1,0:T(8,128)(2,1)S(1)}, u32[]{:S(2)}, u32[]{:S(2)}) collective-permute-start(bf16[4,32,256]{2,1,0:T(8,128)(2,1)S(1)} %slice.83), channel_id=1, source_target_pairs={{0,16},{16,32},{32,48},{48,64},{64,80},{80,96},{96,112},{112,128},... | collective-permute-start | bytes 196616 | tf_op jit(solution)/shard_map/ppermute | solution.py:21
  120.9 10.1 %collective-permute-start.3 = (bf16[16,4,256]{2,1,0:T(4,128)(2,1)S(1)}, bf16[16,4,256]{2,1,0:T(4,128)(2,1)S(1)}, u32[]{:S(2)}, u32[]{:S(2)}) collective-permute-start(bf16[16,4,256]{2,1,0:T(4,128)(2,1)S(1)} %pad_maximum_fusion.6), channel_id=1, source_target_pairs={{0,4},{4,8},{8,12},{12,0},{1,5},{5,9},{9,13},{13,1},{2,6},{6,10},{... | collective-permute-start | bytes 98312 | tf_op jit(solution)/shard_map/ppermute | solution.py:21
  131.1 3.1 copy-start.10
  131.1 2.8 copy-start.12
  133.9 579.8 %reduce-scatter.6.cloned.1.call-start = ((), (), s32[]{:S(2)}) async-start(), calls=%async_computation.6 | async-start | bytes 1310720 | tf_op jit(solution)/shard_map/reduce_scatter | solution.py:91
  134.2 1.9 copy-start.2
  143.0 1.4 copy-start.5
  144.4 13.5 %collective-permute-start.6 = (bf16[4,32,3,256]{3,1,2,0:T(8,128)(2,1)S(1)}, bf16[4,32,3,256]{3,1,2,0:T(8,128)(2,1)S(1)}, u32[]{:S(2)}, u32[]{:S(2)}) collective-permute-start(bf16[4,32,3,256]{3,1,2,0:T(8,128)(2,1)S(1)} %slice.89), channel_id=1, source_target_pairs={{0,16},{16,32},{32,48},{48,64},{64,80},{80,96},{96,112},{112,128},... | collective-permute-start | bytes 589832 | tf_op jit(solution)/shard_map/ppermute | solution.py:21
  158.0 12.4 %copy-start.9 = (bf16[256,1024]{1,0:T(8,128)(2,1)S(1)}, bf16[256,1024]{1,0:T(8,128)(2,1)}, u32[]{:S(2)}) copy-start(bf16[256,1024]{1,0:T(8,128)(2,1)} %param.11) | copy-start | bytes 1572868
  158.0 12.4 %copy-start.13 = (bf16[16,4,256]{2,1,0:T(4,128)(2,1)S(1)}, bf16[16,4,256]{2,1,0:T(4,128)(2,1)}, u32[]{:S(2)}) copy-start(bf16[16,4,256]{2,1,0:T(4,128)(2,1)} %copy-done.12) | copy-start | bytes 98308
  158.0 10.3 %collective-permute-start.7 = (bf16[16,4,3,256]{3,1,2,0:T(4,128)(2,1)S(1)}, bf16[16,4,3,256]{3,1,2,0:T(4,128)(2,1)S(1)}, u32[]{:S(2)}, u32[]{:S(2)}) collective-permute-start(bf16[16,4,3,256]{3,1,2,0:T(4,128)(2,1)S(1)} %pad_maximum_fusion.4), channel_id=1, source_target_pairs={{0,4},{4,8},{8,12},{12,0},{1,5},{5,9},{9,13},{13,1},{2,6},{6,10},{... | collective-permute-start | bytes 294920 | tf_op jit(solution)/shard_map/ppermute | solution.py:21
  170.3 1.7 copy-start.20
  170.3 574.8 %reduce-scatter.4.cloned.1.call-start = ((), (), s32[]{:S(2)}) async-start(), calls=%async_computation.4 | async-start | bytes 1310720 | tf_op jit(solution)/shard_map/reduce_scatter | solution.py:91
  171.8 541.9 %copy-start.1 = (bf16[4,32,1024]{2,1,0:T(8,128)(2,1)S(1)}, bf16[4,32,1024]{2,1,0:T(8,128)(2,1)}, u32[]{:S(2)}) copy-start(bf16[4,32,1024]{2,1,0:T(8,128)(2,1)} %param.7) | copy-start | bytes 786436
  171.8 541.9 %copy-start.15 = (f32[4,32]{1,0:T(4,128)S(1)}, f32[4,32]{1,0:T(4,128)}, u32[]{:S(2)}) copy-start(f32[4,32]{1,0:T(4,128)} %copy-done.14) | copy-start | bytes 1540
  171.8 541.9 %copy-start.16 = (f32[1024]{0:T(1024)S(1)}, f32[1024]{0:T(1024)}, u32[]{:S(2)}) copy-start(f32[1024]{0:T(1024)} %param.9) | copy-start | bytes 12292
  171.8 541.9 %copy-start.18 = (f32[4,32]{1,0:T(4,128)S(1)}, f32[4,32]{1,0:T(4,128)}, u32[]{:S(2)}) copy-start(f32[4,32]{1,0:T(4,128)} %copy-done.17) | copy-start | bytes 1540
  171.9 573.3 %copy-start.7 = (bf16[4,32,1024]{2,1,0:T(8,128)(2,1)S(1)}, bf16[4,32,1024]{2,1,0:T(8,128)(2,1)}, u32[]{:S(2)}) copy-start(bf16[4,32,1024]{2,1,0:T(8,128)(2,1)} %param.13) | copy-start | bytes 786436
  (4 other events, 3.3 us)
Sparse Core Ops, SparseCore 0:
  12.3 33.8 all-gather.2
  48.3 29.6 all-gather.4
  134.0 543.6 reduce-scatter.7
  680.7 33.0 reduce-scatter.5
  716.5 28.6 reduce-scatter.3
